TPU v7x, 32 devices: a whole 2x2x4 slice. The times are simulated.
32 devices in a mesh: frame: 8 (over z, y), head: 2 (over x), batch: 2 (over core).
Axes of the slice: x: 2, y: 2, z: 4, core: 2. Of those that a mesh axis runs over, the one named last changes fastest.
Arguments:
- tokens: bfloat16 [8192, 1536], P(('batch', 'frame')), parts along dimension 0, may hold values from -6 to 6
- query_weight: bfloat16 [1536, 1536], P(None, 'head'), may hold values from -0.15625 to 0.15625
- key_weight: bfloat16 [1536, 1536], P(None, 'head'), may hold values from -0.15625 to 0.15625
- value_weight: bfloat16 [1536, 1536], P(None, 'head'), may hold values from -0.15625 to 0.15625
- out_weight: bfloat16 [1536, 1536], P('head'), may hold values from -0.625 to 0.625
- block_mask: int32 [16, 4, 13], P(('batch', 'frame')), parts along dimension 0, may hold values from 0 to 1, as said below
- frame_level: int32 [64], P(('batch', 'frame')), parts along dimension 0, may hold values from 0 to 15
- modulation: float32 [16, 2, 1536], replicated, may hold values from -1.2 to 13
Outputs:
- layer_out: bfloat16 [8192, 1536], P(('batch', 'frame'), 'head'), parts along dimension 0
There are 2 independent parts, one for each index of `batch`. A program takes and returns all parts, laid end to end along the dimension named above; an argument that names none is the same for every part. Nothing has to cross between parts.
Inputs may be any that keep to these rules, and one draw needn't show every extreme that they name: `block_mask`: in span c every tile with key block below 1, and the tile of query block i with key block (1152) / 128 + i, is always 1; the share of the other tiles that are 1 differs from span to span.
All inputs are finite; a program needn't handle non-finite values.
Results may differ from a plain program's by a relative error of at most 0.01.
The roundings to bfloat16 on the way count: a program that leaves them out, or rounds other values in their place, can miss the bound.
Values may be sent and summed in bfloat16 or wider, within the bound.
A program may use at most 128 MiB of HBM per device.

v0:
```python
import math

import jax
import jax.numpy as jnp
from jax import lax
from jax.sharding import PartitionSpec as P

HEAD_DIM = 128
FRAME_TOK = 128
SINK = 128
TILE = 128


def broadcast(array, axis, root):
    mine = lax.axis_index(axis) == root
    return lax.psum(jnp.where(mine, array, jnp.zeros_like(array)), axis)


def from_behind(array, axis, by):
    length = lax.axis_size(axis)
    pairs = [(i, i + by) for i in range(length) if 0 <= i + by < length]
    return lax.ppermute(array, axis, pairs)


def visible(span_index, span_len, total_keys):
    key_place = jnp.arange(total_keys, dtype=jnp.int32)
    near_start = SINK + span_len
    own_start = SINK + 2 * span_len
    return (
        (key_place < SINK)
        | (key_place >= own_start)
        | (key_place >= near_start) & (span_index >= 1)
        | (key_place < near_start) & (span_index >= 2)
    )


def shards(
    tokens, query_weight, key_weight, value_weight, out_weight, block_mask, frame_level, modulation
):
    span_len, model_width = tokens.shape
    level_count = modulation.shape[0]
    frame_count = frame_level.shape[0]
    xfloat = tokens.astype(jnp.float32)
    mean_square = jnp.mean(xfloat * xfloat, axis=-1, keepdims=True)
    normed = xfloat * lax.rsqrt(mean_square + 1e-06)
    level_onehot = (
        frame_level[:, None] == jnp.arange(level_count, dtype=jnp.int32)[None, :]
    ).astype(jnp.float32)
    chosen = jnp.dot(
        level_onehot,
        modulation.reshape(level_count, 2 * model_width),
        precision=lax.Precision.HIGHEST,
    )
    chosen = chosen.reshape(frame_count, 1, 2, model_width)
    shaped = normed.reshape(frame_count, FRAME_TOK, model_width)
    modulated = (
        (shaped * (1.0 + chosen[:, :, 0]) + chosen[:, :, 1])
        .reshape(span_len, model_width)
        .astype(jnp.bfloat16)
    )
    score_scale = 1.0 / math.sqrt(HEAD_DIM)
    query_rows = (
        jnp.dot(modulated, query_weight, preferred_element_type=jnp.float32) * score_scale
    ).astype(jnp.bfloat16)
    key_value = jnp.stack(
        [
            jnp.dot(modulated, key_weight, preferred_element_type=jnp.float32).astype(jnp.bfloat16),
            jnp.dot(modulated, value_weight, preferred_element_type=jnp.float32).astype(
                jnp.bfloat16
            ),
        ]
    )
    sink_pair = broadcast(key_value[:, :SINK], "frame", 0)
    previous_pair = from_behind(key_value, "frame", 1)
    earlier_pair = from_behind(key_value, "frame", 2)
    window_pair = jnp.concatenate([sink_pair, earlier_pair, previous_pair, key_value], axis=1)
    local_width = query_weight.shape[1]
    local_heads = local_width // HEAD_DIM
    total_keys = window_pair.shape[1]
    key_rows = window_pair[0].reshape(total_keys, local_heads, HEAD_DIM)
    value_rows = window_pair[1].reshape(total_keys, local_heads, HEAD_DIM)
    queries = query_rows.reshape(span_len, local_heads, HEAD_DIM)
    tile_mask = block_mask[0]
    query_blocks, key_blocks = tile_mask.shape
    tile_full = jnp.broadcast_to(
        tile_mask[:, None, :, None], (query_blocks, TILE, key_blocks, TILE)
    ).reshape(span_len, total_keys)
    span_index = lax.axis_index("frame")
    allowed = (tile_full > 0) & visible(span_index, span_len, total_keys)[None, :]
    score_rows = jnp.einsum("qhd,khd->hqk", queries, key_rows, preferred_element_type=jnp.float32)
    masked_scores = jnp.where(allowed[None], score_rows, -1e30)
    row_peak = jnp.max(masked_scores, axis=-1, keepdims=True)
    softmax_num = jnp.where(allowed[None], jnp.exp(masked_scores - row_peak), 0.0)
    row_total = jnp.sum(softmax_num, axis=-1)
    weights_bf = softmax_num.astype(jnp.bfloat16)
    mixed_rows = jnp.einsum(
        "hqk,khd->qhd", weights_bf, value_rows, preferred_element_type=jnp.float32
    )
    attention_out = (
        (mixed_rows / row_total.T[:, :, None]).astype(jnp.bfloat16).reshape(span_len, local_width)
    )
    share_cols = model_width // lax.axis_size("head")
    col_start = lax.axis_index("head") * share_cols
    partial_rows = jnp.dot(attention_out, out_weight, preferred_element_type=jnp.float32)
    summed_rows = lax.psum_scatter(partial_rows, "head", scatter_dimension=1, tiled=True)
    residual_cols = lax.dynamic_slice_in_dim(xfloat, col_start, share_cols, 1)
    return (residual_cols + summed_rows).astype(jnp.bfloat16)


def solution(mesh):
    placed = (
        P(("batch", "frame"), None),
        P(None, "head"),
        P(None, "head"),
        P(None, "head"),
        P("head", None),
        P(("batch", "frame"), None, None),
        P(("batch", "frame")),
        P(),
    )
    return jax.shard_map(
        shards, mesh=mesh, in_specs=placed, out_specs=P(("batch", "frame"), "head"), check_vma=False
    )
```

profile of v0, /device:TPU:14, one launch (start us, length us, event | category | flops | bytes accessed | tf_op | source)
XLA Modules:
  0.0 192.0 jit_solution(17219739829432038658)
XLA Ops:
  6.5 0.0 copy-start
  6.5 0.0 all-reduce.2.cloned.1.call-start
  6.5 0.0 copy-start.1
  6.5 0.0 copy-start.6
  6.5 1.3 convolution_bitcast_fusion
  7.9 1.9 multiply_reduce_fusion
  9.8 0.0 copy-done.1
  9.8 0.5 fusion.8
  10.3 0.0 copy-done.6
  10.3 0.0 copy-start.3
  10.3 0.0 copy-start.7
  10.4 1.4 fusion.15
  11.7 0.0 copy-done.3
  11.8 0.8 copy-done.7
  12.6 1.4 fusion.14
  14.0 0.0 copy-start.2
  14.0 0.9 copy-done.2
  14.8 0.0 copy-start.5
  14.8 1.3 pad_maximum_fusion
  16.2 3.4 %collective-permute-start.1 = (bf16[2,512,768]{2,1,0:T(8,128)(2,1)}, bf16[2,512,768]{2,1,0:T(8,128)(2,1)}, u32[]{:S(2)}, u32[]{:S(2)}) collective-permute-start(bf16[2,512,768]{2,1,0:T(8,128)(2,1)} %pad_maximum_fusion), channel_id=1, source_target_pairs={{0,4},{4,8},{8,12},{12,16},{16,20},{20,24},{24,28},{1,5},{5,9},{9,... | collective-permute-start | bytes 4718600 | tf_op jit(solution)/shard_map/ppermute | solution.py:22
  19.6 3.5 %collective-permute-start = (bf16[2,512,768]{2,1,0:T(8,128)(2,1)}, bf16[2,512,768]{2,1,0:T(8,128)(2,1)}, u32[]{:S(2)}, u32[]{:S(2)}) collective-permute-start(bf16[2,512,768]{2,1,0:T(8,128)(2,1)} %pad_maximum_fusion), channel_id=1, source_target_pairs={{0,8},{4,12},{8,16},{12,20},{16,24},{20,28},{1,9},{5,13},{9,17},{1... | collective-permute-start | bytes 4718600 | tf_op jit(solution)/shard_map/ppermute | solution.py:22
  23.1 1.8 fusion.17
  24.9 0.0 all-reduce.2.cloned.1.call-update
  24.9 0.0 reduce-scatter.2.cloned.1.call-start
  24.9 0.0 copy-done.5
  25.0 0.1 copy.14
  25.1 0.5 broadcast_in_dim.35
  25.6 2.2 %bitcast_and_fusion = pred[512,1664]{0,1:T(8,128)(4,1)} fusion(pred[208,8,4,128]{3,2,1,0:T(4,128)(4,1)S(1)} %bitcast.63, pred[1664]{0:T(1024)(128)(4,1)S(1)} %fusion.23), kind=kLoop, calls=%fused_computation.9 | loop fusion | flops 851968 | bytes 1705600 | tf_op jit(solution)/shard_map/and | solution.py:89
  27.8 3.6 %copy.15 = pred[512,1664]{1,0:T(8,128)(4,1)} copy(pred[512,1664]{0,1:T(8,128)(4,1)} %bitcast_and_fusion) | data formatting | bytes 1703936 | tf_op jit(solution)/shard_map/and | solution.py:89
  31.4 4.4 %multiply_convert_fusion = bf16[512,768]{1,0:T(8,128)(2,1)} fusion(bf16[512,1536]{1,0:T(8,128)(2,1)} %copy-done.3, bf16[1536,768]{1,0:T(8,128)(2,1)} %param.9), kind=kOutput, calls=%fused_computation.22 | convolution fusion | flops 1208745984 | bytes 4718592 | tf_op jit(solution)/shard_map/dot_general | solution.py:63
  35.8 2.3 %copy.16 = bf16[512,768]{0,1:T(8,128)(2,1)} copy(bf16[512,768]{1,0:T(8,128)(2,1)} %multiply_convert_fusion) | data formatting | bytes 1572864 | tf_op jit(solution)/shard_map/convert_element_type | solution.py:64
  38.1 62.3 %all-reduce.2.cloned.1.call-done = bf16[2,128,768]{2,1,0:T(8,128)(2,1)} async-done(((bf16[2,128,768]{2,1,0:T(8,128)(2,1)}), bf16[2,128,768]{2,1,0:T(8,128)(2,1)}) %all-reduce.2.cloned.1.call-update) | async-done | bytes 393232 | tf_op jit(solution)/shard_map/psum | solution.py:16
  100.5 0.0 collective-permute-done.1
  100.5 0.0 collective-permute-done
  100.5 3.0 %maximum_maximum_fusion = bf16[2,1664,768]{2,1,0:T(8,128)(2,1)S(1)} fusion(bf16[1,512,768]{2,1,0:T(8,128)(2,1)S(1)} %fusion.15, bf16[1,512,768]{2,1,0:T(8,128)(2,1)} %copy-done.2, bf16[2,512,768]{2,1,0:T(8,128)(2,1)} %collective-permute-done.1, bf16[2,512,768]{2,1,0:T(8,128)(2,1)} %collective-permute-done, bf16[2,128,768]{2,1,0:T(8,128)(2,1)} %all-reduce.2.cloned.1.call-done), kind=kLoop, calls=%fused_computation.8 | loop fusion | flops 25559040 | bytes 10223616 | tf_op jit(solution)/shard_map/concatenate | solution.py:76
  103.5 2.6 %fusion.30 = (bf16[1,1664,768]{2,1,0:T(8,128)(2,1)}, bf16[1,1664,768]{2,1,0:T(8,128)(2,1)}) fusion(bf16[2,1664,768]{2,1,0:T(8,128)(2,1)S(1)} %maximum_maximum_fusion), kind=kLoop, calls=%fused_computation.49 | loop fusion | bytes 10223616 | tf_op jit(solution)/shard_map/slice | solution.py:80
  106.1 4.5 %copy.13 = bf16[1,1664,768]{1,2,0:T(8,128)(2,1)} copy(bf16[1,1664,768]{2,1,0:T(8,128)(2,1)} %get-tuple-element.6) | data formatting | bytes 5111808 | tf_op jit(solution)/shard_map/slice | solution.py:81
  110.6 0.0 copy-start.4
  110.6 4.6 %copy.17 = bf16[1,1664,768]{1,2,0:T(8,128)(2,1)} copy(bf16[1,1664,768]{2,1,0:T(8,128)(2,1)} %get-tuple-element.5) | data formatting | bytes 5111808 | tf_op jit(solution)/shard_map/slice | solution.py:80
  115.2 0.0 copy-done.4
  115.2 13.3 %fusion.31 = (f32[6,512]{1,0:T(8,128)S(1)}, bf16[6,512,1664]{2,1,0:T(8,128)(2,1)}) fusion(pred[512,1664]{1,0:T(8,128)(4,1)S(1)} %copy-done.4, bf16[512,6,128]{0,2,1:T(8,128)(2,1)} %bitcast.67, bf16[1664,6,128]{0,2,1:T(8,128)(2,1)} %bitcast.65), kind=kOutput, calls=%fused_computation.50 | convolution fusion | flops 1334183552 | bytes 14430208 | tf_op jit(solution)/shard_map/sub | solution.py:93
  128.5 8.1 %fusion.11 = bf16[512,6,128]{0,2,1:T(8,128)(2,1)S(1)} fusion(bf16[1664,6,128]{0,2,1:T(8,128)(2,1)} %bitcast.64, bf16[6,512,1664]{2,1,0:T(8,128)(2,1)} %get-tuple-element.10, f32[512,6]{0,1:T(8,128)S(1)} %bitcast.69), kind=kOutput, calls=%fused_computation.20 | convolution fusion | flops 1309409280 | bytes 13578240 | tf_op jit(solution)/shard_map/hqk,khd->qhd/dot_general | solution.py:96
  136.6 0.0 copy-done
  136.6 3.1 %fusion.32 = f32[512,1536]{1,0:T(8,128)} fusion(bf16[512,768]{0,1:T(8,128)(2,1)S(1)} %bitcast.66, bf16[768,1536]{1,0:T(8,128)(2,1)S(1)} %copy-done), kind=kOutput, calls=%fused_computation.52 | convolution fusion | flops 1207959552 | bytes 6291456 | tf_op jit(solution)/shard_map/dot_general | solution.py:104
  139.7 0.0 reduce-scatter.2.cloned.1.call-update
  139.7 3.5 %convert_element_type.25 = f32[512,1536]{1,0:T(8,128)} convert(bf16[512,1536]{1,0:T(8,128)(2,1)} %param.8) | non-fusion elementwise | flops 786432 | bytes 4718592 | tf_op jit(solution)/shard_map/convert_element_type | solution.py:43
  143.2 39.1 %reduce-scatter.2.cloned.1.call-done = f32[512,768]{1,0:T(8,128)} async-done(((f32[512,1536]{1,0:T(8,128)}), f32[512,768]{1,0:T(8,128)}) %reduce-scatter.2.cloned.1.call-update) | async-done | bytes 1572880 | tf_op jit(solution)/shard_map/reduce_scatter | solution.py:105
  182.2 2.9 %add_convert_fusion = bf16[512,768]{1,0:T(8,128)(2,1)} fusion(f32[512,768]{1,0:T(8,128)} %reduce-scatter.2.cloned.1.call-done, f32[512,1536]{1,0:T(8,128)} %convert_element_type.25, s32[]{:T(128)S(6)} %select_n.18), kind=kLoop, calls=%fused_computation.21 | loop fusion | flops 786432 | bytes 3932164 | tf_op jit(solution)/shard_map/convert_element_type | solution.py:107
  (4 shorter events, 0.0 us)
Async XLA Ops:
  6.5 130.0 %copy-start = (bf16[768,1536]{1,0:T(8,128)(2,1)S(1)}, bf16[768,1536]{1,0:T(8,128)(2,1)}, u32[]{:S(2)}) copy-start(bf16[768,1536]{1,0:T(8,128)(2,1)} %param.12) | copy-start | bytes 7077892
  6.5 93.9 %all-reduce.2.cloned.1.call-start = ((), (), s32[]{:S(2)}) async-start(), calls=%async_computation.1 | async-start | bytes 786432 | tf_op jit(solution)/shard_map/psum | solution.py:16
  6.5 3.2 %copy-start.1 = (bf16[512,1536]{1,0:T(8,128)(2,1)S(1)}, bf16[512,1536]{1,0:T(8,128)(2,1)}, u32[]{:S(2)}) copy-start(bf16[512,1536]{1,0:T(8,128)(2,1)} %param.8) | copy-start | bytes 4718596
  6.5 3.8 %copy-start.6 = (bf16[1536,768]{1,0:T(8,128)(2,1)S(1)}, bf16[1536,768]{1,0:T(8,128)(2,1)}, u32[]{:S(2)}) copy-start(bf16[1536,768]{1,0:T(8,128)(2,1)} %param.11) | copy-start | bytes 7077892
  10.3 1.4 copy-start.3
  10.3 2.2 %copy-start.7 = (bf16[1536,768]{1,0:T(8,128)(2,1)S(1)}, bf16[1536,768]{1,0:T(8,128)(2,1)}, u32[]{:S(2)}) copy-start(bf16[1536,768]{1,0:T(8,128)(2,1)} %param.10) | copy-start | bytes 7077892
  14.0 0.9 copy-start.2
  14.8 10.1 %copy-start.5 = (s32[1,4,13]{2,1,0:T(4,128)S(1)}, s32[1,4,13]{2,1,0:T(4,128)}, u32[]{:S(2)}) copy-start(s32[1,4,13]{2,1,0:T(4,128)} %param.13) | copy-start | bytes 628
  16.2 84.3 %collective-permute-start.1 = (bf16[2,512,768]{2,1,0:T(8,128)(2,1)}, bf16[2,512,768]{2,1,0:T(8,128)(2,1)}, u32[]{:S(2)}, u32[]{:S(2)}) collective-permute-start(bf16[2,512,768]{2,1,0:T(8,128)(2,1)} %pad_maximum_fusion), channel_id=1, source_target_pairs={{0,4},{4,8},{8,12},{12,16},{16,20},{20,24},{24,28},{1,5},{5,9},{9,... | collective-permute-start | bytes 4718600 | tf_op jit(solution)/shard_map/ppermute | solution.py:22
  19.6 80.9 %collective-permute-start = (bf16[2,512,768]{2,1,0:T(8,128)(2,1)}, bf16[2,512,768]{2,1,0:T(8,128)(2,1)}, u32[]{:S(2)}, u32[]{:S(2)}) collective-permute-start(bf16[2,512,768]{2,1,0:T(8,128)(2,1)} %pad_maximum_fusion), channel_id=1, source_target_pairs={{0,8},{4,12},{8,16},{12,20},{16,24},{20,28},{1,9},{5,13},{9,17},{1... | collective-permute-start | bytes 4718600 | tf_op jit(solution)/shard_map/ppermute | solution.py:22
  24.9 157.3 %reduce-scatter.2.cloned.1.call-start = ((), (), s32[]{:S(2)}) async-start(), calls=%async_computation.2 | async-start | bytes 4718592 | tf_op jit(solution)/shard_map/reduce_scatter | solution.py:105
  110.6 4.6 %copy-start.4 = (pred[512,1664]{1,0:T(8,128)(4,1)S(1)}, pred[512,1664]{1,0:T(8,128)(4,1)}, u32[]{:S(2)}) copy-start(pred[512,1664]{1,0:T(8,128)(4,1)} %copy.15) | copy-start | bytes 2555908
Sparse Core Ops, SparseCore 0:
  25.0 75.4 all-reduce.1
  139.8 42.3 reduce-scatter.1
where the time goes:
time: 195 us; the launch traced here: 192 us
  waiting for transfers between devices  101 us (52%)
  matrix products  32.9 us (17%)
  local copies, waits for them, and re-layouts  20 us (10%)
  other arithmetic  17.1 us (9%)
  between operations  13.6 us (7%)
  starting transfers between devices  6.95 us (4%)
    psum x1, waiting for transfers between devices, broadcast(): return lax.psum(jnp.where(mine, array, jnp.zeros_like(array)), axis)  62.3 us
    reduce_scatter x1, waiting for transfers between devices, shards(): lax.psum_scatter(partial_rows, 'head', scatter_dimension=1, tiled=True)  39.1 us
    sub x1, matrix products, shards(): masked_scores - row_peak  13.3 us
    dot_general x1, matrix products, shards(): jnp.einsum('hqk,khd->qhd', weights_bf, value_rows, preferred_element_type...  8.06 us
    slice x2, local copies, waits for them, and re-layouts, shards(): key_rows = window_pair[0].reshape(total_keys, local_heads, HEAD_DIM)  7.2 us
    ppermute x2, starting transfers between devices, from_behind(): return lax.ppermute(array, axis, pairs)  6.9 us
    slice x1, local copies, waits for them, and re-layouts, shards(): value_rows = window_pair[1].reshape(total_keys, local_heads, HEAD_DIM)  4.53 us
    dot_general x1, matrix products, shards(): jnp.dot(modulated, query_weight, preferred_element_type=jnp.float32)  4.4 us
  transfers between devices with their start and end apart: 4, of which 2 were waited for; matrix products, arithmetic and copies ran while one was open for 10% of the time, Pallas kernels for 0%

commit v1 on v0

v1 whole, which is shorter than its diff:
```python
import functools
import math

import jax
import jax.numpy as jnp
from jax import lax
from jax.experimental import pallas as pl
from jax.experimental.pallas import tpu as pltpu
from jax.sharding import PartitionSpec as P

HEAD_DIM = 128
FRAME_TOK = 128
SINK = 128
TILE = 128
CHUNK = 64
DIRECT = 5
MESH = pl.DeviceIdType.MESH


def layer_kernel(
    frames,
    tok_hbm,
    wq_hbm,
    wk_hbm,
    wv_hbm,
    wo_hbm,
    mask_ref,
    level_ref,
    table_ref,
    out_ref,
    tok,
    resid,
    wq,
    wk,
    wv,
    wo_mine,
    wo_theirs,
    own,
    far,
    near,
    sink,
    qbuf,
    kbuf,
    vbuf,
    outgoing,
    incoming,
    kept,
    load_sem,
    sz,
    sy,
    sxf,
    sxn,
    ss,
    rf,
    rn,
    rs,
    so,
    ro,
):
    c = lax.axis_index("frame")
    h = lax.axis_index("head")
    chunks, rows, width = own.shape
    local = wq.shape[1]
    share = out_ref.shape[1]
    heads = local // HEAD_DIM
    span = chunks * rows
    relays = chunks - DIRECT
    even = c % 2 == 0
    total_keys = kbuf.shape[0]
    far_start, near_start, own_start = SINK, SINK + span, SINK + 2 * span

    def load(src, dst, i):
        return pltpu.make_async_copy(src, dst, load_sem.at[i])

    my_cols = pl.ds(pl.multiple_of(h * share, share), share)
    their_cols = pl.ds(pl.multiple_of((1 - h) * share, share), share)
    loads = [
        load(tok_hbm, tok, 0),
        load(wq_hbm, wq, 1),
        load(wk_hbm, wk, 2),
        load(wv_hbm, wv, 3),
        load(wo_hbm.at[:, their_cols], wo_theirs, 4),
        load(wo_hbm.at[:, my_cols], wo_mine, 5),
        load(tok_hbm.at[:, my_cols], resid, 6),
    ]
    for one in loads:
        one.start()

    barrier = pltpu.get_barrier_semaphore()
    pl.semaphore_signal(barrier, inc=1, device_id={"head": 1 - h}, device_id_type=MESH)
    expected = 1
    for step in (1, 2):
        for there, valid in ((c - step, c >= step), (c + step, c + step < frames)):

            @pl.when(valid)
            def _():
                pl.semaphore_signal(
                    barrier, inc=1, device_id={"frame": there}, device_id_type=MESH
                )

            expected = expected + jnp.where(valid, 1, 0)
    pl.semaphore_wait(barrier, expected)

    def place(k):
        return jnp.where(h == 0, k, chunks - 1 - k)

    def remote(src, dst, send, recv, device):
        return pltpu.make_async_remote_copy(
            src_ref=src,
            dst_ref=dst,
            send_sem=send,
            recv_sem=recv,
            device_id=device,
            device_id_type=MESH,
        )

    def z_copy(k):
        i = place(k)
        return remote(own.at[i], far.at[i], sz.at[k], rf.at[i], {"frame": c + 2})

    def y_copy_even(k):
        i = place(k)
        return remote(own.at[i], near.at[i], sy.at[k], rn.at[i], {"frame": c + 1})

    def y_copy_odd(k):
        i = place(k)
        return remote(far.at[i], near.at[i], sy.at[k], rn.at[i], {"frame": c - 1})

    def x_copy_far(k):
        i = place(k)
        return remote(far.at[i], far.at[i], sxf.at[k], rf.at[i], {"head": 1 - h})

    def x_copy_near(k):
        i = place(k)
        return remote(near.at[i], near.at[i], sxn.at[k], rn.at[i], {"head": 1 - h})

    def sink_copy(n, device):
        return remote(sink.at[h], sink.at[h], ss.at[n], rs.at[h], device)

    sink_z = lambda: sink_copy(0, {"frame": c + 2})
    sink_y = lambda: sink_copy(1, {"frame": c + 1})
    sink_x = lambda: sink_copy(2, {"head": 1 - h})
    has_z = c + 2 < frames
    has_far = c >= 2
    has_near = c >= 1

    def modulate(i):
        x = tok[pl.ds(pl.multiple_of(i * rows, rows), rows), :].astype(jnp.float32)
        mean_square = jnp.mean(x * x, axis=-1, keepdims=True)
        normed = x * lax.rsqrt(mean_square + 1e-06)
        level = level_ref[i // (FRAME_TOK // rows)]
        scale_shift = table_ref[level]
        return (normed * (1.0 + scale_shift[0:1]) + scale_shift[1:2]).astype(jnp.bfloat16)

    def send_own(k):
        @pl.when(has_z)
        def _():
            z_copy(k).start()

        @pl.when(even)
        def _():
            y_copy_even(k).start()

    def sink_forward(lo, hi):
        @pl.when((c >= lo) & (c < hi))
        def _():
            sink_z().wait_recv()
            sink_x().start()

            @pl.when(even & has_z)
            def _():
                sink_z().start()

            @pl.when(even)
            def _():
                sink_y().start()

    def far_arrive(k):
        @pl.when(has_far)
        def _():
            z_copy(k).wait_recv()
            if k < relays:
                x_copy_far(k).start()

            @pl.when(jnp.logical_not(even))
            def _():
                y_copy_odd(k).start()

    def near_arrive(k):
        @pl.when(has_near)
        def _():
            y_copy_even(k).wait_recv()
            if k < relays:
                x_copy_near(k).start()

    loads[0].wait()

    @pl.when(c == 0)
    def _():
        for i in range(SINK // rows):
            sink[i] = modulate(i)

        @pl.when(has_z)
        def _():
            sink_z().start()

        sink_y().start()

    early = 2
    for k in range(early):
        own[place(k)] = modulate(place(k))
        send_own(k)

    def rest(k, carry):
        own[place(k)] = modulate(place(k))
        return carry

    lax.fori_loop(early, chunks, rest, 0)

    col_tile = 256

    def project(src, weight, dst, start, count, scale=None):
        flat = src[...].reshape(count, width)

        def tile(n, carry):
            cols = pl.ds(pl.multiple_of(n * col_tile, col_tile), col_tile)
            res = jnp.dot(flat, weight[:, cols], preferred_element_type=jnp.float32)
            if scale is not None:
                res = res * scale
            dst[start : start + count, cols] = res.astype(jnp.bfloat16)
            return carry

        lax.fori_loop(0, local // col_tile, tile, 0)

    loads[1].wait()
    project(own, wq, qbuf, 0, span, 1.0 / math.sqrt(HEAD_DIM))

    sink_forward(1, 3)
    send_own(2)
    far_arrive(0)

    loads[2].wait()
    project(own, wk, kbuf, own_start, span)
    loads[3].wait()
    project(own, wv, vbuf, own_start, span)

    sink_forward(3, 5)
    for k in range(3, DIRECT):
        send_own(k)
    far_arrive(1)
    near_arrive(0)
    far_arrive(2)
    near_arrive(1)
    far_arrive(3)
    near_arrive(2)
    sink_forward(5, frames)
    far_arrive(4)
    near_arrive(3)
    near_arrive(4)

    @pl.when(has_far)
    def _():
        for k in range(DIRECT, chunks):
            remote(
                far.at[place(k)], far.at[place(k)], sxf.at[0], rf.at[place(k)], {"head": 1 - h}
            ).wait_recv()
        project(far, wk, kbuf, far_start, span)
        project(far, wv, vbuf, far_start, span)

    @pl.when(jnp.logical_not(has_far))
    def _():
        kbuf[far_start:near_start, :] = jnp.zeros((span, local), jnp.bfloat16)
        vbuf[far_start:near_start, :] = jnp.zeros((span, local), jnp.bfloat16)

    @pl.when(has_near)
    def _():
        remote(sink.at[1 - h], sink.at[1 - h], ss.at[2], rs.at[1 - h], {"head": 1 - h}).wait_recv()

    project(sink, wk, kbuf, 0, SINK)
    project(sink, wv, vbuf, 0, SINK)

    @pl.when(has_near)
    def _():
        for k in range(DIRECT, chunks):
            remote(
                near.at[place(k)], near.at[place(k)], sxn.at[0], rn.at[place(k)], {"head": 1 - h}
            ).wait_recv()
        project(near, wk, kbuf, near_start, span)
        project(near, wv, vbuf, near_start, span)

    @pl.when(jnp.logical_not(has_near))
    def _():
        kbuf[near_start:own_start, :] = jnp.zeros((span, local), jnp.bfloat16)
        vbuf[near_start:own_start, :] = jnp.zeros((span, local), jnp.bfloat16)

    for i in (4, 5, 6):
        loads[i].wait()

    key_blocks = total_keys // TILE
    far_ok = jnp.where(has_far, 1, 0)
    near_ok = jnp.where(has_near, 1, 0)

    def out_copy(b):
        return remote(outgoing.at[b], incoming.at[b], so.at[b], ro.at[b], {"head": 1 - h})

    def query_block(b, carry):
        q_rows = pl.ds(pl.multiple_of(b * TILE, TILE), TILE)
        parts = []
        for j in range(key_blocks):
            seen = mask_ref[b, j]
            if far_start <= j * TILE < near_start:
                seen = seen * far_ok
            elif near_start <= j * TILE < own_start:
                seen = seen * near_ok
            parts.append(jnp.full((1, TILE), jnp.where(seen > 0, 0.0, -1e30), jnp.float32))
        bias = jnp.concatenate(parts, axis=1)
        mixed = []
        for n in range(heads):
            cols = slice(n * HEAD_DIM, (n + 1) * HEAD_DIM)
            scores = lax.dot_general(
                qbuf[q_rows, cols],
                kbuf[:, cols],
                (((1,), (1,)), ((), ())),
                preferred_element_type=jnp.float32,
            )
            scores = scores + bias
            peak = jnp.max(scores, axis=-1, keepdims=True)
            num = jnp.exp(scores - peak)
            total = jnp.sum(num, axis=-1, keepdims=True)
            rows_out = jnp.dot(
                num.astype(jnp.bfloat16), vbuf[:, cols], preferred_element_type=jnp.float32
            )
            mixed.append((rows_out / total).astype(jnp.bfloat16))
        attended = jnp.concatenate(mixed, axis=1)
        outgoing[b] = jnp.dot(
            attended, wo_theirs[...], preferred_element_type=jnp.float32
        ).astype(jnp.bfloat16)
        out_copy(b).start()
        kept[b] = resid[q_rows, :].astype(jnp.float32) + jnp.dot(
            attended, wo_mine[...], preferred_element_type=jnp.float32
        )
        return carry

    blocks = span // TILE
    lax.fori_loop(0, blocks, query_block, 0)

    def finish(b, carry):
        q_rows = pl.ds(pl.multiple_of(b * TILE, TILE), TILE)
        out_copy(b).wait_recv()
        out_ref[q_rows, :] = (kept[b] + incoming[b].astype(jnp.float32)).astype(jnp.bfloat16)
        return carry

    lax.fori_loop(0, blocks, finish, 0)

    def finish_send(b, carry):
        out_copy(b).wait_send()
        return carry

    lax.fori_loop(0, blocks, finish_send, 0)

    for k in range(DIRECT):

        @pl.when(has_z)
        def _():
            z_copy(k).wait_send()

        @pl.when(even)
        def _():
            y_copy_even(k).wait_send()

        @pl.when(jnp.logical_not(even) & has_far)
        def _():
            y_copy_odd(k).wait_send()

    for k in range(relays):

        @pl.when(has_far)
        def _():
            x_copy_far(k).wait_send()

        @pl.when(has_near)
        def _():
            x_copy_near(k).wait_send()

    @pl.when(even & has_z)
    def _():
        sink_z().wait_send()

    @pl.when(even)
    def _():
        sink_y().wait_send()

    @pl.when(has_near)
    def _():
        sink_x().wait_send()


def shards(
    tokens, query_weight, key_weight, value_weight, out_weight, block_mask, frame_level, modulation
):
    span, width = tokens.shape
    local = query_weight.shape[1]
    share = width // lax.axis_size("head")
    chunks = span // CHUNK
    relays = chunks - DIRECT
    blocks = span // TILE
    total_keys = SINK + 3 * span
    bf16, f32 = jnp.bfloat16, jnp.float32
    dma = pltpu.SemaphoreType.DMA
    anywhere = pl.BlockSpec(memory_space=pl.ANY)
    smem = pl.BlockSpec(memory_space=pltpu.SMEM)
    vmem = pl.BlockSpec(memory_space=pltpu.VMEM)
    return pl.pallas_call(
        functools.partial(layer_kernel, lax.axis_size("frame")),
        out_shape=jax.ShapeDtypeStruct((span, share), bf16),
        in_specs=[anywhere] * 5 + [smem, smem, vmem],
        out_specs=vmem,
        scratch_shapes=[
            pltpu.VMEM((span, width), bf16),
            pltpu.VMEM((span, share), bf16),
            pltpu.VMEM((width, local), bf16),
            pltpu.VMEM((width, local), bf16),
            pltpu.VMEM((width, local), bf16),
            pltpu.VMEM((local, share), bf16),
            pltpu.VMEM((local, share), bf16),
            pltpu.VMEM((chunks, CHUNK, width), bf16),
            pltpu.VMEM((chunks, CHUNK, width), bf16),
            pltpu.VMEM((chunks, CHUNK, width), bf16),
            pltpu.VMEM((SINK // CHUNK, CHUNK, width), bf16),
            pltpu.VMEM((span, local), bf16),
            pltpu.VMEM((total_keys, local), bf16),
            pltpu.VMEM((total_keys, local), bf16),
            pltpu.VMEM((blocks, TILE, share), bf16),
            pltpu.VMEM((blocks, TILE, share), bf16),
            pltpu.VMEM((blocks, TILE, share), f32),
            dma((7,)),
            dma((DIRECT,)),
            dma((DIRECT,)),
            dma((relays,)),
            dma((relays,)),
            dma((3,)),
            dma((chunks,)),
            dma((chunks,)),
            dma((2,)),
            dma((blocks,)),
            dma((blocks,)),
        ],
        compiler_params=pltpu.CompilerParams(
            collective_id=0, has_side_effects=True, vmem_limit_bytes=60 * 1024 * 1024
        ),
        name="layer",
    )(
        tokens,
        query_weight,
        key_weight,
        value_weight,
        out_weight,
        block_mask[0],
        frame_level,
        modulation,
    )


def solution(mesh):
    placed = (
        P(("batch", "frame"), None),
        P(None, "head"),
        P(None, "head"),
        P(None, "head"),
        P("head", None),
        P(("batch", "frame"), None, None),
        P(("batch", "frame")),
        P(),
    )
    return jax.shard_map(
        shards, mesh=mesh, in_specs=placed, out_specs=P(("batch", "frame"), "head"), check_vma=False
    )
```

time: 195 us -> 70.2 us (0.36); the launches traced: 192 us -> 70 us
  waiting for transfers between devices: 101 us -> 0 us
  Pallas kernels: 0 us -> 67.9 us
  matrix products: 32.9 us -> 0 us
  local copies, waits for them, and re-layouts: 20 us -> 2.06 us
  other arithmetic: 17.1 us -> 0 us
  between operations: 13.6 us -> 0.01 us
  starting transfers between devices: 6.95 us -> 0 us
    pallas_call x0 -> x1, Pallas kernels: none -> 67.9 us  [shards(): pl.pallas_call(functools.partial(layer_kernel, lax.axis_size('frame')), o...]
    psum x1 -> x0, waiting for transfers between devices: 62.3 us -> none  [broadcast(): return lax.psum(jnp.where(mine, array, jnp.zeros_like(array)), axis)]
    reduce_scatter x1 -> x0, waiting for transfers between devices: 39.1 us -> none  [shards(): lax.psum_scatter(partial_rows, 'head', scatter_dimension=1, tiled=True)]
    dot_general x6 -> x0, matrix products: 19.6 us -> none  [the longest x1 8.06 us: shards(): jnp.einsum('hqk,khd->qhd', weights_bf, value_rows, preferred_element_type...]
    sub x1 -> x0, matrix products: 13.3 us -> none  [shards(): masked_scores - row_peak]
    slice x3 -> x0, local copies, waits for them, and re-layouts: 11.7 us -> none  [the longest x2 7.2 us: shards(): key_rows = window_pair[0].reshape(total_keys, local_heads, HEAD_DIM)]
    convert_element_type x3 -> x0, other arithmetic: 6.92 us -> none  [the longest x1 3.49 us: shards(): xfloat = tokens.astype(jnp.float32)]
    ppermute x2 -> x0, starting transfers between devices: 6.9 us -> none  [from_behind(): return lax.ppermute(array, axis, pairs)]
  transfers between devices with their start and end apart: 4 -> 0, of which waited for: 2 -> 0; matrix products, arithmetic and copies ran while one was open for 10% -> 0% of each run, Pallas kernels for 0% -> 0%
where the time goes in v1:
time: 70.2 us; the launch traced here: 70 us
  Pallas kernels  67.9 us (97%)
  local copies, waits for them, and re-layouts  2.06 us (3%)
    pallas_call x1, Pallas kernels, shards(): pl.pallas_call(functools.partial(layer_kernel, lax.axis_size('frame')), o...  67.9 us
    unnamed x1, local copies, waits for them, and re-layouts  2.06 us

profile of v1, /device:TPU:14, one launch (start us, length us, event | category | flops | bytes accessed | tf_op | source)
XLA Modules:
  0.0 70.0 jit_solution(3681185807318079748)
XLA Ops:
  0.0 67.9 %layer.1 = bf16[512,768]{1,0:T(8,128)(2,1)} custom-call(bf16[512,1536]{1,0:T(8,128)(2,1)} %tok_hbm.1, bf16[1536,768]{1,0:T(8,128)(2,1)} %wq_hbm.1, bf16[1536,768]{1,0:T(8,128)(2,1)} %wk_hbm.1, bf16[1536,768]{1,0:T(8,128)(2,1)} %wv_hbm.1, bf16[768,1536]{1,0:T(8,128)(2,1)} %wo_hbm.1, s32[4,13]{1,0:T(4,128)} %bitcast.1, s32[4]{0:T(128)} %level_ref.1, ...), custom_call_target="tpu_custom_call" | custom-call | tf_op jit(solution)/shard_map/layer/pallas_call | solution.py:413
  67.9 2.1 %copy.10 = bf16[512,768]{1,0:T(8,128)(2,1)} copy(bf16[512,768]{1,0:T(8,128)(2,1)} %layer.1) | data formatting | bytes 1572864

commit v2 on v1

--- a/solution.py
+++ b/solution.py
@@ -13,7 +13,7 @@
 SINK = 128
 TILE = 128
 CHUNK = 64
-DIRECT = 5
+DIRECT = 6
 MESH = pl.DeviceIdType.MESH
 
 
@@ -161,19 +161,22 @@
         def _():
             y_copy_even(k).start()
 
-    def sink_forward(lo, hi):
-        @pl.when((c >= lo) & (c < hi))
+    def sink_even(lo, hi):
+        @pl.when(even & (c >= lo) & (c < hi))
         def _():
             sink_z().wait_recv()
             sink_x().start()
-
-            @pl.when(even & has_z)
+            sink_y().start()
+
+            @pl.when(has_z)
             def _():
                 sink_z().start()
 
-            @pl.when(even)
-            def _():
-                sink_y().start()
+    def sink_odd():
+        @pl.when(jnp.logical_not(even))
+        def _():
+            sink_z().wait_recv()
+            sink_x().start()
 
     def far_arrive(k):
         @pl.when(has_far)
@@ -219,79 +222,100 @@
 
     col_tile = 256
 
-    def project(src, weight, dst, start, count, scale=None):
-        flat = src[...].reshape(count, width)
+    def project(src, weight, dst, start, scale=None):
+        flat = src[...].reshape(-1, width)
+        count = flat.shape[0]
+        if not isinstance(start, int):
+            start = pl.multiple_of(start, TILE)
 
         def tile(n, carry):
             cols = pl.ds(pl.multiple_of(n * col_tile, col_tile), col_tile)
             res = jnp.dot(flat, weight[:, cols], preferred_element_type=jnp.float32)
             if scale is not None:
                 res = res * scale
-            dst[start : start + count, cols] = res.astype(jnp.bfloat16)
+            dst[pl.ds(start, count), cols] = res.astype(jnp.bfloat16)
             return carry
 
         lax.fori_loop(0, local // col_tile, tile, 0)
 
+    half = chunks // 2
+
+    def project_half(src, start, which):
+        piece = src.at[pl.ds(which * half, half)]
+        project(piece, wk, kbuf, start + which * half * rows)
+        project(piece, wv, vbuf, start + which * half * rows)
+
+    def relayed_wait(buf, send, recv):
+        for k in range(DIRECT, chunks):
+            i = place(k)
+            remote(buf.at[i], buf.at[i], send.at[0], recv.at[i], {"head": 1 - h}).wait_recv()
+
     loads[1].wait()
-    project(own, wq, qbuf, 0, span, 1.0 / math.sqrt(HEAD_DIM))
-
-    sink_forward(1, 3)
+    project(own, wq, qbuf, 0, 1.0 / math.sqrt(HEAD_DIM))
+
+    sink_even(2, 3)
     send_own(2)
     far_arrive(0)
 
     loads[2].wait()
-    project(own, wk, kbuf, own_start, span)
+    project(own, wk, kbuf, own_start)
     loads[3].wait()
-    project(own, wv, vbuf, own_start, span)
-
-    sink_forward(3, 5)
-    for k in range(3, DIRECT):
-        send_own(k)
+    project(own, wv, vbuf, own_start)
+
+    sink_even(4, 5)
+    send_own(3)
     far_arrive(1)
     near_arrive(0)
     far_arrive(2)
     near_arrive(1)
+    sink_even(6, frames)
+    for k in range(4, DIRECT):
+        send_own(k)
     far_arrive(3)
     near_arrive(2)
-    sink_forward(5, frames)
+
+    @pl.when(has_far)
+    def _():
+        project_half(far, far_start, h)
+
+    @pl.when(jnp.logical_not(has_far))
+    def _():
+        kbuf[far_start:near_start, :] = jnp.zeros((span, local), jnp.bfloat16)
+        vbuf[far_start:near_start, :] = jnp.zeros((span, local), jnp.bfloat16)
+
     far_arrive(4)
     near_arrive(3)
-    near_arrive(4)
-
-    @pl.when(has_far)
-    def _():
-        for k in range(DIRECT, chunks):
-            remote(
-                far.at[place(k)], far.at[place(k)], sxf.at[0], rf.at[place(k)], {"head": 1 - h}
-            ).wait_recv()
-        project(far, wk, kbuf, far_start, span)
-        project(far, wv, vbuf, far_start, span)
-
-    @pl.when(jnp.logical_not(has_far))
-    def _():
-        kbuf[far_start:near_start, :] = jnp.zeros((span, local), jnp.bfloat16)
-        vbuf[far_start:near_start, :] = jnp.zeros((span, local), jnp.bfloat16)
 
     @pl.when(has_near)
     def _():
-        remote(sink.at[1 - h], sink.at[1 - h], ss.at[2], rs.at[1 - h], {"head": 1 - h}).wait_recv()
-
-    project(sink, wk, kbuf, 0, SINK)
-    project(sink, wv, vbuf, 0, SINK)
-
-    @pl.when(has_near)
-    def _():
-        for k in range(DIRECT, chunks):
-            remote(
-                near.at[place(k)], near.at[place(k)], sxn.at[0], rn.at[place(k)], {"head": 1 - h}
-            ).wait_recv()
-        project(near, wk, kbuf, near_start, span)
-        project(near, wv, vbuf, near_start, span)
+        project_half(near, near_start, h)
 
     @pl.when(jnp.logical_not(has_near))
     def _():
         kbuf[near_start:own_start, :] = jnp.zeros((span, local), jnp.bfloat16)
         vbuf[near_start:own_start, :] = jnp.zeros((span, local), jnp.bfloat16)
+
+    sink_odd()
+    far_arrive(5)
+    near_arrive(4)
+
+    @pl.when(has_far)
+    def _():
+        relayed_wait(far, sxf, rf)
+        project_half(far, far_start, 1 - h)
+
+    @pl.when(has_near)
+    def _():
+        remote(sink.at[1 - h], sink.at[1 - h], ss.at[2], rs.at[1 - h], {"head": 1 - h}).wait_recv()
+
+    project(sink, wk, kbuf, 0)
+    project(sink, wv, vbuf, 0)
+    near_arrive(5)
+
+    @pl.when(has_near)
+    def _():
+        relayed_wait(near, sxn, rn)
+        project_half(near, near_start, 1 - h)
 
     for i in (4, 5, 6):
         loads[i].wait()

time: 70.2 us -> 64.5 us (0.919)
  the two profiles are of different devices: /device:TPU:14 before, /device:TPU:8 now
where the time goes in v2:
time: 64.5 us; the launch traced here: 64.4 us
  Pallas kernels  62.3 us (97%)
  local copies, waits for them, and re-layouts  2.06 us (3%)
    pallas_call x1, Pallas kernels, shards(): pl.pallas_call(functools.partial(layer_kernel, lax.axis_size('frame')), o...  62.3 us
    unnamed x1, local copies, waits for them, and re-layouts  2.06 us

profile of v2, /device:TPU:8, one launch (start us, length us, event | category | flops | bytes accessed | tf_op | source)
XLA Modules:
  0.0 64.4 jit_solution(5967207094846025219)
XLA Ops:
  0.0 62.3 %layer.1 = bf16[512,768]{1,0:T(8,128)(2,1)} custom-call(bf16[512,1536]{1,0:T(8,128)(2,1)} %tok_hbm.1, bf16[1536,768]{1,0:T(8,128)(2,1)} %wq_hbm.1, bf16[1536,768]{1,0:T(8,128)(2,1)} %wk_hbm.1, bf16[1536,768]{1,0:T(8,128)(2,1)} %wv_hbm.1, bf16[768,1536]{1,0:T(8,128)(2,1)} %wo_hbm.1, s32[4,13]{1,0:T(4,128)} %bitcast.1, s32[4]{0:T(128)} %level_ref.1, ...), custom_call_target="tpu_custom_call" | custom-call | tf_op jit(solution)/shard_map/layer/pallas_call | solution.py:437
  62.3 2.1 %copy.10 = bf16[512,768]{1,0:T(8,128)(2,1)} copy(bf16[512,768]{1,0:T(8,128)(2,1)} %layer.1) | data formatting | bytes 1572864
